TPU v7x, 32 devices: a whole 2x2x4 slice. The times are simulated.
32 devices in a mesh: group: 4 (over y, x), slot: 8 (over z, core).
Axes of the slice: x: 2, y: 2, z: 4, core: 2. Of those that a mesh axis runs over, the one named last changes fastest.
Arguments:
- tokens: bfloat16 [4096, 2048], P(('group', 'slot')), may hold values from -6 to 6
- cotangent: bfloat16 [4096, 512], P(('group', 'slot')), may hold values from -0.59765625 to 0.59765625
- weight_halves: bfloat16 [32, 1024, 512], P(('group', 'slot')), may hold values from -0.125 to 0.125
- momentum_halves: bfloat16 [32, 1024, 512], P(('group', 'slot')), may hold values from -6 to 6
- old_map: int32 [4, 4], replicated, may hold values from 0 to 3, each once within a row
- new_map: int32 [4, 8], replicated, may hold values from 0 to 3, as said below
- row_ids: int32 [32, 128], P(('group', 'slot')), may hold values from 0 to 127
Outputs:
- projected: bfloat16 [4096, 512], P(('group', 'slot'))
Inputs may be any that keep to these rules, and one draw needn't show every extreme that they name: `old_map`: each row names each of the group's experts once. `new_map`: every expert is hosted by one to four new slots; among the experts of every owner group one is hosted by exactly four.
All inputs are finite; a program needn't handle non-finite values.
Results may differ from a plain program's by a relative error of at most 0.007.
Values may be sent and summed in bfloat16 or wider, within the bound.
No kernel may reach another device: no remote copies, remote signals or barrier semaphores. Data moves between devices by JAX's collectives and lax.ppermute only.
A program may use at most 64 MiB of HBM per device.

v0:
```python
import math
import jax
import jax.numpy as jnp
from jax import lax
from jax.sharding import PartitionSpec as P

ITERS = 2
coef_a = 3.4445
coef_b = -4.775
coef_c = 2.0315
momentum_rate = 0.95
step_scale = 0.01
gram_eps = 1e-06
contract_rows = (((0,), (0,)), ((), ()))


def swapped(shard, axis, stride):
    return lax.ppermute(shard, axis, [(i, i ^ 1 << stride) for i in range(lax.axis_size(axis))])


def pick_columns(token_block, which_half, slot_count):
    row_count, col_count = token_block.shape
    pieces_view = token_block.reshape(row_count, slot_count, 2, col_count // (2 * slot_count))
    chosen = lax.dynamic_index_in_dim(pieces_view, which_half, axis=2, keepdims=False)
    return chosen.reshape(row_count, col_count // 2)


def inner_gram(half_rows):
    return lax.dot_general(
        half_rows, half_rows, contract_rows, preferred_element_type=jnp.float32
    ).astype(jnp.bfloat16)


def make_polynomial(scaled):
    gram_bf = scaled.astype(jnp.bfloat16)
    square = jnp.dot(gram_bf, gram_bf, preferred_element_type=jnp.float32)
    return (coef_b * scaled + coef_c * square).astype(jnp.bfloat16)


def on_device(tokens, cotangent, weight_halves, momentum_halves, old_map, new_map, row_ids):
    slot_count = lax.axis_size("slot")
    host_count = slot_count // lax.axis_size("group")
    model_width = tokens.shape[1]
    hidden = cotangent.shape[1]
    half_index = lax.axis_index("slot") % 2
    group_id = lax.axis_index("group")
    outgoing = jnp.concatenate(
        [pick_columns(tokens, 1 - half_index, slot_count), cotangent], axis=1
    )
    incoming = swapped(outgoing, "slot", 0)
    own_term = lax.dot_general(
        pick_columns(tokens, half_index, slot_count),
        cotangent,
        contract_rows,
        preferred_element_type=jnp.float32,
    ).astype(jnp.bfloat16)
    peer_term = lax.dot_general(
        incoming[:, : model_width // 2],
        incoming[:, model_width // 2 :],
        contract_rows,
        preferred_element_type=jnp.float32,
    ).astype(jnp.bfloat16)
    gradient = own_term.astype(jnp.float32) + peer_term.astype(jnp.float32)
    current = (momentum_rate * momentum_halves[0].astype(jnp.float32) + gradient).astype(
        jnp.bfloat16
    )
    own_gram = inner_gram(current)
    for iteration in range(ITERS):
        peer_gram = swapped(own_gram, "slot", 0)
        gram_sum = own_gram.astype(jnp.float32) + peer_gram.astype(jnp.float32)
        if iteration == 0:
            norm_sq = jnp.trace(gram_sum) + gram_eps
            gram_sum = gram_sum / norm_sq
            factor = 1.0 / jnp.sqrt(norm_sq)
        else:
            factor = 1.0
        polynomial = make_polynomial(gram_sum)
        product = jnp.dot(current, polynomial, preferred_element_type=jnp.float32)
        current = (factor * (coef_a * current.astype(jnp.float32) + product)).astype(jnp.bfloat16)
        if iteration + 1 < ITERS:
            own_gram = inner_gram(current)
    renewed = (
        weight_halves[0].astype(jnp.float32)
        - step_scale * math.sqrt(model_width) * current.astype(jnp.float32)
    ).astype(jnp.bfloat16)
    blocks = lax.all_to_all(
        renewed.reshape(slot_count, -1, hidden), "slot", split_axis=0, concat_axis=0, tiled=True
    )
    pieces = blocks.reshape(slot_count // 2, -1, hidden)
    requests = lax.dynamic_slice_in_dim(new_map, group_id * host_count, host_count, axis=1).reshape(
        -1
    )
    own_list = lax.dynamic_index_in_dim(old_map, group_id, 0, keepdims=False)
    holder = jnp.argmax((own_list[None, :] == requests[:, None]).astype(jnp.int32), axis=1)
    outgoing_blocks = jnp.take(pieces, holder, axis=0)
    weight_new = lax.all_to_all(
        lax.all_to_all(outgoing_blocks, "group", split_axis=0, concat_axis=0, tiled=True),
        "slot",
        split_axis=0,
        concat_axis=1,
        tiled=True,
    )[0]
    chosen = jnp.take(tokens, row_ids[0], axis=0)
    return jnp.dot(chosen, weight_new, preferred_element_type=jnp.float32).astype(jnp.bfloat16)


def solution(mesh):
    placed = (
        P(("group", "slot"), None),
        P(("group", "slot"), None),
        P(("group", "slot"), None, None),
        P(("group", "slot"), None, None),
        P(),
        P(),
        P(("group", "slot"), None),
    )
    return jax.shard_map(
        on_device, mesh=mesh, in_specs=placed, out_specs=P(("group", "slot"), None), check_vma=False
    )
```

profile of v0, /device:TPU:0, one launch (start us, length us, event | category | flops | bytes accessed | tf_op | source)
XLA Modules:
  0.0 131.6 jit_solution(12882281342114190404)
XLA Ops:
  0.0 1.4 %copy.11 = bf16[128,2048]{0,1:T(8,128)(2,1)S(1)} copy(bf16[128,2048]{1,0:T(8,128)(2,1)} %param.7) | data formatting | bytes 1048576 | tf_op args[0]
  1.4 1.0 copy.12
  2.5 0.6 collective-permute-start
  3.5 0.9 collective-permute-done
  4.5 0.5 fusion.1
  5.0 0.7 convolution_convert_fusion.3
  5.7 0.4 collective-permute-start.1
  6.2 1.5 %collective-permute-done.1 = bf16[512,512]{1,0:T(8,128)(2,1)S(1)} collective-permute-done((bf16[512,512]{1,0:T(8,128)(2,1)S(1)}, bf16[512,512]{1,0:T(8,128)(2,1)S(1)}, u32[]{:S(2)}, u32[]{:S(2)}) %collective-permute-start.1) | collective-permute-done | bytes 524320 | tf_op jit(solution)/shard_map/ppermute | solution.py:18
  7.7 0.7 select_reduce_fusion
  9.1 1.2 multiply_convert_fusion
  10.3 0.7 convolution_convert_fusion.2
  11.0 0.4 collective-permute-start.2
  11.4 1.5 %collective-permute-done.2 = bf16[512,512]{1,0:T(8,128)(2,1)S(1)} collective-permute-done((bf16[512,512]{1,0:T(8,128)(2,1)S(1)}, bf16[512,512]{1,0:T(8,128)(2,1)S(1)}, u32[]{:S(2)}, u32[]{:S(2)}) %collective-permute-start.2) | collective-permute-done | bytes 524320 | tf_op jit(solution)/shard_map/ppermute | solution.py:18
  13.0 2.3 %fusion = bf16[1024,512]{1,0:T(8,128)(2,1)} fusion(bf16[1024,512]{1,0:T(8,128)(2,1)S(1)} %multiply_convert_fusion, bf16[1,1024,512]{2,1,0:T(8,128)(2,1)S(1)} %copy-done.4, bf16[512,512]{1,0:T(8,128)(2,1)S(1)} %collective-permute-done.2, bf16[512,512]{1,0:T(8,128)(2,1)S(1)} %convolution_convert_fusion.2), kind=kOutput, calls=%fused_computation.3 | convolution fusion | flops 812908544 | bytes 4194304 | tf_op jit(solution)/shard_map/dot_general | solution.py:78
  15.3 6.2 %all-to-all-start = ((bf16[8,128,512]{2,1,0:T(8,128)(2,1)}), bf16[8,128,512]{2,1,0:T(8,128)(2,1)S(1)}, u32[]{:S(2)}, u32[]{:S(2)}) async-start(bf16[8,128,512]{2,1,0:T(8,128)(2,1)} %bitcast.9), calls=%async_computation | async-start | bytes 2097152 | tf_op jit(solution)/shard_map/all_to_all | solution.py:86
  21.7 0.7 fusion.24
  22.3 0.6 iota_reduce_fusion
  23.0 25.1 %all-to-all-done = bf16[8,128,512]{2,1,0:T(8,128)(2,1)S(1)} async-done(((bf16[8,128,512]{2,1,0:T(8,128)(2,1)}), bf16[8,128,512]{2,1,0:T(8,128)(2,1)S(1)}, u32[]{:S(2)}, u32[]{:S(2)}) %all-to-all-start) | async-done | bytes 1048608 | tf_op jit(solution)/shard_map/all_to_all | solution.py:86
  48.0 0.7 gather_fusion.1
  49.0 28.7 %all_to_all.19 = bf16[8,256,512]{2,1,0:T(8,128)(2,1)} all-to-all(bf16[8,256,512]{2,1,0:T(8,128)(2,1)S(1)} %broadcast_select_fusion), channel_id=1, replica_groups=mesh['group'=4,'slot'=8] {'group'}, dimensions={0} | all-to-all | bytes 4194304 | tf_op jit(solution)/shard_map/all_to_all | solution.py:97
  77.7 3.7 %all-to-all-start.2 = ((bf16[8,256,512]{2,1,0:T(8,128)(2,1)}), bf16[8,256,512]{2,1,0:T(8,128)(2,1)S(1)}, u32[]{:S(2)}, u32[]{:S(2)}) async-start(bf16[8,256,512]{2,1,0:T(8,128)(2,1)} %all_to_all.19), calls=%async_computation.2 | async-start | bytes 4194304 | tf_op jit(solution)/shard_map/all_to_all | solution.py:96
  81.5 0.9 gather_fusion
  82.5 48.0 %all-to-all-done.2 = bf16[8,256,512]{2,1,0:T(8,128)(2,1)S(1)} async-done(((bf16[8,256,512]{2,1,0:T(8,128)(2,1)}), bf16[8,256,512]{2,1,0:T(8,128)(2,1)S(1)}, u32[]{:S(2)}, u32[]{:S(2)}) %all-to-all-start.2) | async-done | bytes 2097184 | tf_op jit(solution)/shard_map/all_to_all | solution.py:96
  130.4 1.1 convolution_convert_fusion.4
  (24 shorter events, 1.0 us)
Async XLA Ops:
  0.0 21.5 %copy-start = (s32[4,8]{1,0:T(4,128)S(1)}, s32[4,8]{1,0:T(4,128)}, u32[]{:S(2)}) copy-start(s32[4,8]{1,0:T(4,128)} %param.12) | copy-start | bytes 388
  0.0 3.1 %copy-start.3 = (bf16[128,512]{1,0:T(8,128)(2,1)S(1)}, bf16[128,512]{1,0:T(8,128)(2,1)}, u32[]{:S(2)}) copy-start(bf16[128,512]{1,0:T(8,128)(2,1)} %param.8) | copy-start | bytes 393220
  0.0 4.5 %copy-start.2 = (bf16[1,1024,512]{2,1,0:T(8,128)(2,1)S(1)}, bf16[1,1024,512]{2,1,0:T(8,128)(2,1)}, u32[]{:S(2)}) copy-start(bf16[1,1024,512]{2,1,0:T(8,128)(2,1)} %param.10) | copy-start | bytes 3145732
  2.5 1.9 %collective-permute-start = (bf16[128,1536]{0,1:T(8,128)(2,1)S(1)}, bf16[128,1536]{0,1:T(8,128)(2,1)S(1)}, u32[]{:S(2)}, u32[]{:S(2)}) collective-permute-start(bf16[128,1536]{0,1:T(8,128)(2,1)S(1)} %pad_maximum_fusion), channel_id=1, source_target_pairs={{0,1},{1,0},{2,3},{3,2},{4,5},{5,4},{6,7},{7,6},{8,9},{9,8},{10,11... | collective-permute-start | bytes 1179656 | tf_op jit(solution)/shard_map/ppermute | solution.py:18
  5.7 2.0 %collective-permute-start.1 = (bf16[512,512]{1,0:T(8,128)(2,1)S(1)}, bf16[512,512]{1,0:T(8,128)(2,1)S(1)}, u32[]{:S(2)}, u32[]{:S(2)}) collective-permute-start(bf16[512,512]{1,0:T(8,128)(2,1)S(1)} %convolution_convert_fusion.3), channel_id=1, source_target_pairs={{0,1},{1,0},{2,3},{3,2},{4,5},{5,4},{6,7},{7,6},{8,9},{9,8},{10,11... | collective-permute-start | bytes 1572872 | tf_op jit(solution)/shard_map/ppermute | solution.py:18
  10.3 2.7 %copy-start.4 = (bf16[1,1024,512]{2,1,0:T(8,128)(2,1)S(1)}, bf16[1,1024,512]{2,1,0:T(8,128)(2,1)}, u32[]{:S(2)}) copy-start(bf16[1,1024,512]{2,1,0:T(8,128)(2,1)} %param.9) | copy-start | bytes 3145732
  11.0 2.0 %collective-permute-start.2 = (bf16[512,512]{1,0:T(8,128)(2,1)S(1)}, bf16[512,512]{1,0:T(8,128)(2,1)S(1)}, u32[]{:S(2)}, u32[]{:S(2)}) collective-permute-start(bf16[512,512]{1,0:T(8,128)(2,1)S(1)} %convolution_convert_fusion.2), channel_id=1, source_target_pairs={{0,1},{1,0},{2,3},{3,2},{4,5},{5,4},{6,7},{7,6},{8,9},{9,8},{10,11... | collective-permute-start | bytes 1572872 | tf_op jit(solution)/shard_map/ppermute | solution.py:18
  15.3 32.8 %all-to-all-start = ((bf16[8,128,512]{2,1,0:T(8,128)(2,1)}), bf16[8,128,512]{2,1,0:T(8,128)(2,1)S(1)}, u32[]{:S(2)}, u32[]{:S(2)}) async-start(bf16[8,128,512]{2,1,0:T(8,128)(2,1)} %bitcast.9), calls=%async_computation | async-start | bytes 2097152 | tf_op jit(solution)/shard_map/all_to_all | solution.py:86
  77.7 3.7 %copy-start.5 = (s32[1,128]{1,0:T(1,128)S(1)}, s32[1,128]{1,0:T(1,128)}, u32[]{:S(2)}) copy-start(s32[1,128]{1,0:T(1,128)} %param.13) | copy-start | bytes 1540
  77.7 3.8 %copy-start.1 = (bf16[128,2048]{1,0:T(8,128)(2,1)S(1)}, bf16[128,2048]{1,0:T(8,128)(2,1)}, u32[]{:S(2)}) copy-start(bf16[128,2048]{1,0:T(8,128)(2,1)} %param.7) | copy-start | bytes 1572868
  77.7 52.7 %all-to-all-start.2 = ((bf16[8,256,512]{2,1,0:T(8,128)(2,1)}), bf16[8,256,512]{2,1,0:T(8,128)(2,1)S(1)}, u32[]{:S(2)}, u32[]{:S(2)}) async-start(bf16[8,256,512]{2,1,0:T(8,128)(2,1)} %all_to_all.19), calls=%async_computation.2 | async-start | bytes 4194304 | tf_op jit(solution)/shard_map/all_to_all | solution.py:96
where the time goes:
time: 132 us
  waiting for transfers between devices  77.1 us (58%)
  blocking collectives  28.7 us (22%)
  starting transfers between devices  11.4 us (9%)
  matrix products  7.01 us (5%)
  local copies, waits for them, and re-layouts  4.96 us (4%)
  other arithmetic  1.6 us (1%)
    all_to_all x1, waiting for transfers between devices, on_device(): lax.all_to_all(lax.all_to_all(outgoing_blocks, 'group', split_axis=0, con...  48 us
    all_to_all x1, blocking collectives, on_device(): lax.all_to_all(outgoing_blocks, 'group', split_axis=0, concat_axis=0, til...  28.7 us
    all_to_all x1, waiting for transfers between devices, on_device(): lax.all_to_all(renewed.reshape(slot_count, -1, hidden), 'slot', split_axi...  25.1 us
    all_to_all x1, starting transfers between devices, on_device(): lax.all_to_all(renewed.reshape(slot_count, -1, hidden), 'slot', split_axi...  6.22 us
    ppermute x3, waiting for transfers between devices, swapped(): lax.ppermute(shard, axis, [(i, i ^ 1 << stride) for i in range(lax.axis_s...  4.01 us
    all_to_all x1, starting transfers between devices, on_device(): lax.all_to_all(lax.all_to_all(outgoing_blocks, 'group', split_axis=0, con...  3.73 us
    dot_general x2, matrix products, on_device(): product = jnp.dot(current, polynomial, preferred_element_type=jnp.float32)  3.44 us
  transfers between devices with their start and end apart: 5, of which 5 were waited for; matrix products, arithmetic and copies ran while one was open for 2% of the time, Pallas kernels for 0%

commit v1 on v0

--- a/solution.py
+++ b/solution.py
@@ -93,12 +93,23 @@
     own_list = lax.dynamic_index_in_dim(old_map, group_id, 0, keepdims=False)
     holder = jnp.argmax((own_list[None, :] == requests[:, None]).astype(jnp.int32), axis=1)
     outgoing_blocks = jnp.take(pieces, holder, axis=0)
-    weight_new = lax.all_to_all(
-        lax.all_to_all(outgoing_blocks, "group", split_axis=0, concat_axis=0, tiled=True),
-        "slot",
-        split_axis=0,
-        concat_axis=1,
-        tiled=True,
+    weight_new = jnp.concatenate(
+        lax.all_to_all(
+            jnp.stack(
+                jnp.split(
+                    lax.all_to_all(
+                        outgoing_blocks, "group", split_axis=0, concat_axis=0, tiled=True
+                    ),
+                    lax.psum(1, "slot"),
+                    0,
+                ),
+                axis=0,
+            ),
+            "slot",
+            0,
+            0,
+        ),
+        1,
     )[0]
     chosen = jnp.take(tokens, row_ids[0], axis=0)
     return jnp.dot(chosen, weight_new, preferred_element_type=jnp.float32).astype(jnp.bfloat16)

time: 132 us -> 138 us (1.045)
  local copies, waits for them, and re-layouts: 4.96 us -> 10.7 us
    unnamed x14 -> x21, local copies, waits for them, and re-layouts: 2.46 us -> 7.5 us
where the time goes in v1:
time: 138 us; the launch traced here: 137 us
  waiting for transfers between devices  77.1 us (56%)
  blocking collectives  28.6 us (21%)
  starting transfers between devices  11.4 us (8%)
  local copies, waits for them, and re-layouts  10.7 us (8%)
  matrix products  7.02 us (5%)
  other arithmetic  1.6 us (1%)
    all_to_all x1, waiting for transfers between devices, on_device(): lax.all_to_all(jnp.stack(jnp.split(lax.all_to_all(outgoing_blocks, 'group...  48 us
    all_to_all x1, blocking collectives, on_device(): lax.all_to_all(outgoing_blocks, 'group', split_axis=0, concat_axis=0, til...  28.6 us
    all_to_all x1, waiting for transfers between devices, on_device(): lax.all_to_all(renewed.reshape(slot_count, -1, hidden), 'slot', split_axi...  25.1 us
    unnamed x21, local copies, waits for them, and re-layouts  7.5 us
    all_to_all x1, starting transfers between devices, on_device(): lax.all_to_all(renewed.reshape(slot_count, -1, hidden), 'slot', split_axi...  6.22 us
    ppermute x3, waiting for transfers between devices, swapped(): lax.ppermute(shard, axis, [(i, i ^ 1 << stride) for i in range(lax.axis_s...  4.01 us
    all_to_all x1, starting transfers between devices, on_device(): lax.all_to_all(jnp.stack(jnp.split(lax.all_to_all(outgoing_blocks, 'group...  3.73 us
    dot_general x2, matrix products, on_device(): product = jnp.dot(current, polynomial, preferred_element_type=jnp.float32)  3.44 us
  transfers between devices with their start and end apart: 5, of which 5 were waited for; matrix products, arithmetic and copies ran while one was open for 2% of the time, Pallas kernels for 0%

profile of v1, /device:TPU:0, one launch (start us, length us, event | category | flops | bytes accessed | tf_op | source)
XLA Modules:
  0.0 137.2 jit_solution(13862555449779576536)
XLA Ops:
  0.0 1.4 %copy.11 = bf16[128,2048]{0,1:T(8,128)(2,1)S(1)} copy(bf16[128,2048]{1,0:T(8,128)(2,1)} %param.7) | data formatting | bytes 1048576 | tf_op args[0]
  1.4 1.0 copy.12
  3.5 0.9 collective-permute-done
  5.0 0.7 convolution_convert_fusion.3
  6.2 1.5 %collective-permute-done.1 = bf16[512,512]{1,0:T(8,128)(2,1)S(1)} collective-permute-done((bf16[512,512]{1,0:T(8,128)(2,1)S(1)}, bf16[512,512]{1,0:T(8,128)(2,1)S(1)}, u32[]{:S(2)}, u32[]{:S(2)}) %collective-permute-start.1) | collective-permute-done | bytes 524320 | tf_op jit(solution)/shard_map/ppermute | solution.py:18
  9.1 1.2 multiply_convert_fusion
  10.3 0.7 convolution_convert_fusion.2
  11.4 1.5 %collective-permute-done.2 = bf16[512,512]{1,0:T(8,128)(2,1)S(1)} collective-permute-done((bf16[512,512]{1,0:T(8,128)(2,1)S(1)}, bf16[512,512]{1,0:T(8,128)(2,1)S(1)}, u32[]{:S(2)}, u32[]{:S(2)}) %collective-permute-start.2) | collective-permute-done | bytes 524320 | tf_op jit(solution)/shard_map/ppermute | solution.py:18
  13.0 2.3 %fusion = bf16[1024,512]{1,0:T(8,128)(2,1)} fusion(bf16[1024,512]{1,0:T(8,128)(2,1)S(1)} %multiply_convert_fusion, bf16[1,1024,512]{2,1,0:T(8,128)(2,1)S(1)} %copy-done.4, bf16[512,512]{1,0:T(8,128)(2,1)S(1)} %collective-permute-done.2, bf16[512,512]{1,0:T(8,128)(2,1)S(1)} %convolution_convert_fusion.2), kind=kOutput, calls=%fused_computation.3 | convolution fusion | flops 812908544 | bytes 4194304 | tf_op jit(solution)/shard_map/dot_general | solution.py:78
  15.3 6.2 %all-to-all-start = ((bf16[8,128,512]{2,1,0:T(8,128)(2,1)}), bf16[8,128,512]{2,1,0:T(8,128)(2,1)S(1)}, u32[]{:S(2)}, u32[]{:S(2)}) async-start(bf16[8,128,512]{2,1,0:T(8,128)(2,1)} %bitcast.9), calls=%async_computation | async-start | bytes 2097152 | tf_op jit(solution)/shard_map/all_to_all | solution.py:86
  23.0 25.1 %all-to-all-done = bf16[8,128,512]{2,1,0:T(8,128)(2,1)S(1)} async-done(((bf16[8,128,512]{2,1,0:T(8,128)(2,1)}), bf16[8,128,512]{2,1,0:T(8,128)(2,1)S(1)}, u32[]{:S(2)}, u32[]{:S(2)}) %all-to-all-start) | async-done | bytes 1048608 | tf_op jit(solution)/shard_map/all_to_all | solution.py:86
  49.0 28.6 %all_to_all.15 = bf16[8,256,512]{2,1,0:T(8,128)(2,1)S(1)} all-to-all(bf16[8,256,512]{2,1,0:T(8,128)(2,1)S(1)} %broadcast_select_fusion), channel_id=1, replica_groups=mesh['group'=4,'slot'=8] {'group'}, dimensions={0} | all-to-all | bytes 4194304 | tf_op jit(solution)/shard_map/all_to_all | solution.py:100
  77.6 0.7 fusion.28
  78.3 0.7 fusion.27
  79.0 0.7 fusion.26
  79.7 0.7 fusion.25
  80.5 0.7 fusion.24
  81.2 0.7 fusion.23
  81.9 0.7 fusion.22
  82.7 0.7 fusion.21
  83.4 3.7 %all-to-all-start.2 = ((bf16[8,1,256,512]{3,2,1,0:T(8,128)(2,1)}), bf16[8,1,256,512]{3,2,1,0:T(8,128)(2,1)S(1)}, u32[]{:S(2)}, u32[]{:S(2)}) async-start(bf16[8,1,256,512]{3,2,1,0:T(8,128)(2,1)} %fusion.21), calls=%async_computation.2 | async-start | bytes 4194304 | tf_op jit(solution)/shard_map/all_to_all | solution.py:97
  87.2 0.9 gather_fusion
  88.1 48.0 %all-to-all-done.2 = bf16[8,1,256,512]{3,2,1,0:T(8,128)(2,1)S(1)} async-done(((bf16[8,1,256,512]{3,2,1,0:T(8,128)(2,1)}), bf16[8,1,256,512]{3,2,1,0:T(8,128)(2,1)S(1)}, u32[]{:S(2)}, u32[]{:S(2)}) %all-to-all-start.2) | async-done | bytes 2097184 | tf_op jit(solution)/shard_map/all_to_all | solution.py:97
  136.1 1.2 convolution_convert_fusion.4
  (32 shorter events, 5.6 us)
Async XLA Ops:
  0.0 21.5 %copy-start = (s32[4,8]{1,0:T(4,128)S(1)}, s32[4,8]{1,0:T(4,128)}, u32[]{:S(2)}) copy-start(s32[4,8]{1,0:T(4,128)} %param.12) | copy-start | bytes 388
  0.0 3.1 %copy-start.3 = (bf16[128,512]{1,0:T(8,128)(2,1)S(1)}, bf16[128,512]{1,0:T(8,128)(2,1)}, u32[]{:S(2)}) copy-start(bf16[128,512]{1,0:T(8,128)(2,1)} %param.8) | copy-start | bytes 393220
  0.0 4.5 %copy-start.2 = (bf16[1,1024,512]{2,1,0:T(8,128)(2,1)S(1)}, bf16[1,1024,512]{2,1,0:T(8,128)(2,1)}, u32[]{:S(2)}) copy-start(bf16[1,1024,512]{2,1,0:T(8,128)(2,1)} %param.10) | copy-start | bytes 3145732
  2.5 1.9 %collective-permute-start = (bf16[128,1536]{0,1:T(8,128)(2,1)S(1)}, bf16[128,1536]{0,1:T(8,128)(2,1)S(1)}, u32[]{:S(2)}, u32[]{:S(2)}) collective-permute-start(bf16[128,1536]{0,1:T(8,128)(2,1)S(1)} %pad_maximum_fusion), channel_id=1, source_target_pairs={{0,1},{1,0},{2,3},{3,2},{4,5},{5,4},{6,7},{7,6},{8,9},{9,8},{10,11... | collective-permute-start | bytes 1179656 | tf_op jit(solution)/shard_map/ppermute | solution.py:18
  5.7 2.0 %collective-permute-start.1 = (bf16[512,512]{1,0:T(8,128)(2,1)S(1)}, bf16[512,512]{1,0:T(8,128)(2,1)S(1)}, u32[]{:S(2)}, u32[]{:S(2)}) collective-permute-start(bf16[512,512]{1,0:T(8,128)(2,1)S(1)} %convolution_convert_fusion.3), channel_id=1, source_target_pairs={{0,1},{1,0},{2,3},{3,2},{4,5},{5,4},{6,7},{7,6},{8,9},{9,8},{10,11... | collective-permute-start | bytes 1572872 | tf_op jit(solution)/shard_map/ppermute | solution.py:18
  10.3 2.7 %copy-start.4 = (bf16[1,1024,512]{2,1,0:T(8,128)(2,1)S(1)}, bf16[1,1024,512]{2,1,0:T(8,128)(2,1)}, u32[]{:S(2)}) copy-start(bf16[1,1024,512]{2,1,0:T(8,128)(2,1)} %param.9) | copy-start | bytes 3145732
  11.0 2.0 %collective-permute-start.2 = (bf16[512,512]{1,0:T(8,128)(2,1)S(1)}, bf16[512,512]{1,0:T(8,128)(2,1)S(1)}, u32[]{:S(2)}, u32[]{:S(2)}) collective-permute-start(bf16[512,512]{1,0:T(8,128)(2,1)S(1)} %convolution_convert_fusion.2), channel_id=1, source_target_pairs={{0,1},{1,0},{2,3},{3,2},{4,5},{5,4},{6,7},{7,6},{8,9},{9,8},{10,11... | collective-permute-start | bytes 1572872 | tf_op jit(solution)/shard_map/ppermute | solution.py:18
  15.3 32.8 %all-to-all-start = ((bf16[8,128,512]{2,1,0:T(8,128)(2,1)}), bf16[8,128,512]{2,1,0:T(8,128)(2,1)S(1)}, u32[]{:S(2)}, u32[]{:S(2)}) async-start(bf16[8,128,512]{2,1,0:T(8,128)(2,1)} %bitcast.9), calls=%async_computation | async-start | bytes 2097152 | tf_op jit(solution)/shard_map/all_to_all | solution.py:86
  83.4 3.7 %copy-start.5 = (s32[1,128]{1,0:T(1,128)S(1)}, s32[1,128]{1,0:T(1,128)}, u32[]{:S(2)}) copy-start(s32[1,128]{1,0:T(1,128)} %param.13) | copy-start | bytes 1540
  83.4 3.8 %copy-start.1 = (bf16[128,2048]{1,0:T(8,128)(2,1)S(1)}, bf16[128,2048]{1,0:T(8,128)(2,1)}, u32[]{:S(2)}) copy-start(bf16[128,2048]{1,0:T(8,128)(2,1)} %param.7) | copy-start | bytes 1572868
  83.4 52.7 %all-to-all-start.2 = ((bf16[8,1,256,512]{3,2,1,0:T(8,128)(2,1)}), bf16[8,1,256,512]{3,2,1,0:T(8,128)(2,1)S(1)}, u32[]{:S(2)}, u32[]{:S(2)}) async-start(bf16[8,1,256,512]{3,2,1,0:T(8,128)(2,1)} %fusion.21), calls=%async_computation.2 | async-start | bytes 4194304 | tf_op jit(solution)/shard_map/all_to_all | solution.py:97
